TPU v7x, 512 devices: a whole 4x4x16 slice. The times are simulated.
512 devices in a mesh: loop: 32 (over x, z_lo, core), grp: 16 (over z_hi, y).
Axes of the slice: x: 4, y: 4, z: 16 (z_hi: 4, z_lo: 4; z = z_hi * 4 + z_lo), core: 2. Of those that a mesh axis runs over, the one named last changes fastest.
Arguments:
- adjacency_tiles: bfloat16 [65536, 128, 128], P(('loop', 'grp')), may hold values from -0.046875 to 0.046875
- row_block: int32 [65536], P(('loop', 'grp')), may hold values from 0 to 31
- column_block: int32 [65536], P(('loop', 'grp')), may hold values from 0 to 15
- features: bfloat16 [65536, 256], P(('loop', 'grp')), may hold values from -6 to 6
- weight: bfloat16 [256, 256], replicated, may hold values from -0.375 to 0.375
- out_bias: float32 [256], replicated, may hold values from -3 to 3
Outputs:
- result: bfloat16 [65536, 256], P(('loop', 'grp'))
All inputs are finite; a program needn't handle non-finite values.
Results may differ from a plain program's by a relative error of at most 0.0046.
Values may be sent and summed in bfloat16 or wider, within the bound.
No kernel may reach another device: no remote copies, remote signals or barrier semaphores. Data moves between devices by JAX's collectives and lax.ppermute only.
A program may use at most 128 MiB of HBM per device.

v0:
```python
import jax
import jax.numpy as jnp
from jax import lax
from jax.sharding import PartitionSpec as P


def on_device(adjacency_tiles, row_block, column_block, features, weight, out_bias):
    tile_size = adjacency_tiles.shape[1]
    feat_width = features.shape[1]
    loop_count = lax.axis_size("loop")
    section_rows = lax.all_gather(features, "grp", axis=0, tiled=True)
    section_blocks = section_rows.reshape(-1, tile_size, feat_width)
    picked = jnp.take(section_blocks, column_block, axis=0)
    products = jnp.einsum(
        "tij,tjf->tif", adjacency_tiles, picked, preferred_element_type=jnp.float32
    )
    partial_value = jax.ops.segment_sum(products, row_block, num_segments=loop_count)
    summed = lax.psum_scatter(partial_value, "loop", scatter_dimension=0, tiled=True)
    aggregate = summed.reshape(tile_size, feat_width).astype(jnp.bfloat16)
    mixed = jnp.dot(aggregate, weight, preferred_element_type=jnp.float32) + out_bias
    return jax.nn.relu(mixed).astype(jnp.bfloat16)


def solution(mesh):
    in_specs = (
        P(("loop", "grp"), None, None),
        P(("loop", "grp")),
        P(("loop", "grp")),
        P(("loop", "grp"), None),
        P(),
        P(),
    )
    out_specs = P(("loop", "grp"), None)
    return jax.shard_map(
        on_device, mesh=mesh, in_specs=in_specs, out_specs=out_specs, check_vma=False
    )
```

profile of v0, /device:TPU:1, one launch (start us, length us, event | category | flops | bytes accessed | tf_op | source)
XLA Modules:
  0.0 329.4 jit_solution(5589250887956877626)
XLA Ops:
  6.5 0.0 copy-start
  6.5 0.0 all-gather.2.cloned.1.call-start
  6.5 0.7 all-gather.2.cloned.1.call-update
  7.3 0.0 reduce-scatter.2.cloned.1.call-start
  7.3 0.7 compare_select_fusion
  8.0 0.7 compare_and_fusion
  8.6 84.2 %all-gather.2.cloned.1.call-done = bf16[2048,256]{1,0:T(8,128)(2,1)} async-done(((bf16[128,256]{1,0:T(8,128)(2,1)}), bf16[2048,256]{1,0:T(8,128)(2,1)}) %all-gather.2.cloned.1.call-update) | async-done | bytes 1048592 | tf_op jit(solution)/shard_map/all_gather | solution.py:11
  92.9 7.8 %gather_fusion = bf16[128,128,256]{2,1,0:T(8,128)(2,1)} fusion(bf16[16,128,256]{2,1,0:T(8,128)(2,1)} %bitcast.8, s32[1024]{0:T(1024)S(1)} %pad_clamp_fusion), kind=kCustom, calls=%fused_computation | custom fusion | bytes 16777728 | tf_op jit(solution)/shard_map/jit(_take)/gather | solution.py:13
  100.6 13.1 %convolution_bitcast_fusion = f32[128,128,256]{1,2,0:T(8,128)} fusion(bf16[128,128,128]{2,1,0:T(8,128)(2,1)} %param.6, bf16[128,128,256]{2,1,0:T(8,128)(2,1)} %gather_fusion, pred[128]{0:T(512)(128)(4,1)S(1)} %compare_and_fusion), kind=kOutput, calls=%fused_computation.2 | convolution fusion | flops 1077936128 | bytes 29360256 | tf_op jit(solution)/shard_map/tij,tjf->tif/dot_general | solution.py:14
  113.8 0.0 copy-start.2
  113.8 17.5 %copy.9 = f32[128,128,256]{2,1,0:T(8,128)} copy(f32[128,128,256]{1,2,0:T(8,128)} %convolution_bitcast_fusion) | data formatting | bytes 33554432 | tf_op jit(solution)/shard_map/tij,tjf->tif/dot_general | solution.py:14
  131.2 2.4 broadcast_in_dim.19
  133.6 0.0 copy-done.2
  133.6 0.0 copy-start.1
  133.6 37.6 %scatter_fusion = f32[32,128,256]{2,1,0:T(8,128)} fusion(f32[32,128,256]{2,1,0:T(8,128)} %broadcast_in_dim.19, s32[128]{0:T(128)S(1)} %copy-done.2, f32[128,128,256]{2,1,0:T(8,128)} %copy.9), kind=kCustom, calls=%fused_computation.1 | custom fusion | flops 4194304 | bytes 50332160 | tf_op jit(solution)/shard_map/scatter-add | solution.py:17
  171.3 0.0 reduce-scatter.2.cloned.1.call-update
  171.3 149.6 %reduce-scatter.2.cloned.1.call-done = f32[1,128,256]{2,1,0:T(8,128)} async-done(((f32[32,128,256]{2,1,0:T(8,128)}), f32[1,128,256]{2,1,0:T(8,128)}) %reduce-scatter.2.cloned.1.call-update) | async-done | bytes 131088 | tf_op jit(solution)/shard_map/reduce_scatter | solution.py:18
  320.9 0.0 copy-done
  320.9 0.0 copy-done.1
  320.9 1.7 fusion.4
  (1 shorter events, 0.0 us)
Async XLA Ops:
  6.5 314.4 %copy-start = (bf16[256,256]{1,0:T(8,128)(2,1)S(1)}, bf16[256,256]{1,0:T(8,128)(2,1)}, u32[]{:S(2)}) copy-start(bf16[256,256]{1,0:T(8,128)(2,1)} %param.10) | copy-start | bytes 393220
  6.5 86.3 %all-gather.2.cloned.1.call-start = ((), (), s32[]{:S(2)}) async-start(), calls=%async_computation.1 | async-start | bytes 1114112 | tf_op jit(solution)/shard_map/all_gather | solution.py:11
  7.3 313.6 %reduce-scatter.2.cloned.1.call-start = ((), (), s32[]{:S(2)}) async-start(), calls=%async_computation.2 | async-start | bytes 4325376 | tf_op jit(solution)/shard_map/reduce_scatter | solution.py:18
  113.8 19.9 %copy-start.2 = (s32[128]{0:T(128)S(1)}, s32[128]{0:T(128)}, u32[]{:S(2)}) copy-start(s32[128]{0:T(128)} %param.7) | copy-start | bytes 1540
  133.6 187.3 %copy-start.1 = (f32[256]{0:T(256)S(1)}, f32[256]{0:T(256)}, u32[]{:S(2)}) copy-start(f32[256]{0:T(256)} %param.11) | copy-start | bytes 3076
Sparse Core Ops, SparseCore 0:
  10.3 82.4 all-gather.1
  171.4 149.4 reduce-scatter.1
where the time goes:
time: 334 us; the launch traced here: 329 us
  waiting for transfers between devices  235 us (70%)
  other arithmetic  39 us (12%)
  local copies, waits for them, and re-layouts  27.7 us (8%)
  matrix products  14.8 us (4%)
  between operations  13.4 us (4%)
    reduce_scatter x1, waiting for transfers between devices, on_device(): lax.psum_scatter(partial_value, 'loop', scatter_dimension=0, tiled=True)  150 us
    all_gather x1, waiting for transfers between devices, on_device(): section_rows = lax.all_gather(features, 'grp', axis=0, tiled=True)  84.2 us
    scatter-add x1, other arithmetic, on_device(): jax.ops.segment_sum(products, row_block, num_segments=loop_count)  37.6 us
    dot_general x1, local copies, waits for them, and re-layouts, on_device(): jnp.einsum('tij,tjf->tif', adjacency_tiles, picked, preferred_element_typ...  17.5 us
    dot_general x1, matrix products, on_device(): jnp.einsum('tij,tjf->tif', adjacency_tiles, picked, preferred_element_typ...  13.1 us
    gather x1, local copies, waits for them, and re-layouts, on_device(): picked = jnp.take(section_blocks, column_block, axis=0)  7.78 us
  transfers between devices with their start and end apart: 2, of which 2 were waited for; matrix products, arithmetic and copies ran while one was open for 0% of the time, Pallas kernels for 0%

commit v1 on v0

v1 whole, which is shorter than its diff:
```python
import functools

import jax
import jax.numpy as jnp
from jax import lax
from jax.experimental import pallas as pl
from jax.experimental.pallas import tpu as pltpu
from jax.sharding import Mesh, PartitionSpec as P

F32 = jnp.float32
BF16 = jnp.bfloat16
GROUP = 32
VMEM_LIMIT = 20 << 20


def tile_kernel(group, core_ref, rows_ref, cols_ref, adj_ref, feat_ref, own_ref, other_ref, acc):
    step = pl.program_id(0)
    half = own_ref.shape[0]
    core = core_ref[0]

    @pl.when(step == 0)
    def _():
        acc[...] = jnp.zeros_like(acc)

    for k in range(group):
        t = step * group + k
        row = rows_ref[t]
        col = cols_ref[t]
        slot = ((row & 1) ^ core) * half + (row >> 1)
        block = (col & 3) * 4 + (col >> 2)
        acc[slot] += jnp.dot(adj_ref[k], feat_ref[block], preferred_element_type=F32)

    @pl.when(step == pl.num_programs(0) - 1)
    def _():
        own_ref[...] = acc[:half]
        other_ref[...] = acc[half:].astype(BF16)


def tile_products(core, rows, cols, tiles, section):
    count, side, _ = tiles.shape
    width = section.shape[2]
    half = 16
    return pl.pallas_call(
        functools.partial(tile_kernel, GROUP),
        out_shape=(
            jax.ShapeDtypeStruct((half, side, width), F32),
            jax.ShapeDtypeStruct((half, side, width), BF16),
        ),
        grid_spec=pltpu.PrefetchScalarGridSpec(
            num_scalar_prefetch=3,
            grid=(count // GROUP,),
            in_specs=[
                pl.BlockSpec((GROUP, side, side), lambda i, *_: (i, 0, 0)),
                pl.BlockSpec(memory_space=pltpu.VMEM),
            ],
            out_specs=(pl.BlockSpec(memory_space=pltpu.VMEM),) * 2,
            scratch_shapes=[pltpu.VMEM((2 * half, side, width), F32)],
        ),
        cost_estimate=pl.CostEstimate(
            flops=2 * count * side * side * width,
            bytes_accessed=tiles.size * 2,
            transcendentals=0,
        ),
        compiler_params=pltpu.CompilerParams(vmem_limit_bytes=VMEM_LIMIT),
        name="tile_products",
    )(core, rows, cols, tiles, section)


def gather_blocks(blocks, axis):
    n = lax.axis_size(axis)
    copies = jnp.broadcast_to(blocks[None], (n,) + blocks.shape)
    copies = copies.reshape((-1,) + blocks.shape[1:])
    return lax.all_to_all(copies, axis, 0, 0, tiled=True)


def sum_scatter(blocks, axis):
    n = lax.axis_size(axis)
    arrived = lax.all_to_all(blocks, axis, 0, 0, tiled=True)
    parts = arrived.reshape((n, -1) + blocks.shape[1:]).astype(F32)
    total = parts[0]
    for i in range(1, n):
        total = total + parts[i]
    return total


def on_device(adjacency_tiles, row_block, column_block, features, weight, out_bias):
    core = lax.axis_index("c")
    section = gather_blocks(gather_blocks(features[None], "zh"), "y")
    own, other = tile_products(
        core.reshape(1).astype(jnp.int32), row_block, column_block, adjacency_tiles, section
    )
    received = lax.ppermute(other, "c", [(0, 1), (1, 0)])
    chip = (own + received.astype(F32)).astype(BF16)
    plane = sum_scatter(chip, "x").astype(BF16)
    aggregate = sum_scatter(plane, "zl")[0].astype(BF16)
    mixed = jnp.dot(aggregate, weight, preferred_element_type=F32) + out_bias
    return jax.nn.relu(mixed).astype(BF16)


def solution(mesh):
    fine = Mesh(mesh.devices.reshape(4, 4, 2, 4, 4), ("x", "zl", "c", "zh", "y"))
    every = ("x", "zl", "c", "zh", "y")
    in_specs = (P(every, None, None), P(every), P(every), P(every, None), P(), P())
    return jax.shard_map(
        on_device, mesh=fine, in_specs=in_specs, out_specs=P(every, None), check_vma=False
    )
```

time: 334 us -> 98.7 us (0.30)
  waiting for transfers between devices: 235 us -> 12 us
  blocking collectives: 0 us -> 62.1 us
  other arithmetic: 39 us -> 0.72 us
  local copies, waits for them, and re-layouts: 27.7 us -> 4.17 us
  matrix products: 14.8 us -> 0.8 us
  between operations: 13.4 us -> 0.08 us
  starting transfers between devices: 0.04 us -> 13 us
  Pallas kernels: 0 us -> 4.07 us
    reduce_scatter x1 -> x0, waiting for transfers between devices: 150 us -> none  [on_device(): lax.psum_scatter(partial_value, 'loop', scatter_dimension=0, tiled=True)]
    all_gather x1 -> x0, waiting for transfers between devices: 84.2 us -> none  [on_device(): section_rows = lax.all_gather(features, 'grp', axis=0, tiled=True)]
    all_to_all x0 -> x3, blocking collectives: none -> 62.1 us  [the longest x2 32.5 us: sum_scatter(): arrived = lax.all_to_all(blocks, axis, 0, 0, tiled=True)]
    scatter-add x1 -> x0, other arithmetic: 37.6 us -> none  [on_device(): jax.ops.segment_sum(products, row_block, num_segments=loop_count)]
    dot_general x1 -> x0, local copies, waits for them, and re-layouts: 17.5 us -> none  [on_device(): jnp.einsum('tij,tjf->tif', adjacency_tiles, picked, preferred_element_typ...]
    dot_general x2 -> x1, matrix products: 14.8 us -> 0.8 us  [on_device(): mixed = jnp.dot(aggregate, weight, preferred_element_type=F32) + out_bias]
    all_to_all x0 -> x1, waiting for transfers between devices: none -> 9.74 us  [gather_blocks(): return lax.all_to_all(copies, axis, 0, 0, tiled=True)]
    ppermute x0 -> x1, starting transfers between devices: none -> 8.81 us  [on_device(): received = lax.ppermute(other, 'c', [(0, 1), (1, 0)])]
where the time goes in v1:
time: 98.7 us; the launch traced here: 96.9 us
  blocking collectives  62.1 us (63%)
  starting transfers between devices  13 us (13%)
  waiting for transfers between devices  12 us (12%)
  local copies, waits for them, and re-layouts  4.17 us (4%)
  Pallas kernels  4.07 us (4%)
    all_to_all x2, blocking collectives, sum_scatter(): arrived = lax.all_to_all(blocks, axis, 0, 0, tiled=True)  32.5 us
    all_to_all x1, blocking collectives, gather_blocks(): return lax.all_to_all(copies, axis, 0, 0, tiled=True)  29.6 us
    all_to_all x1, waiting for transfers between devices, gather_blocks(): return lax.all_to_all(copies, axis, 0, 0, tiled=True)  9.74 us
    ppermute x1, starting transfers between devices, on_device(): received = lax.ppermute(other, 'c', [(0, 1), (1, 0)])  8.81 us
    all_to_all x1, starting transfers between devices, gather_blocks(): return lax.all_to_all(copies, axis, 0, 0, tiled=True)  4.18 us
    pallas_call x1, Pallas kernels, tile_products(): pl.pallas_call(functools.partial(tile_kernel, GROUP), out_shape=(jax.Shap...  4.07 us
    ppermute x1, waiting for transfers between devices, on_device(): received = lax.ppermute(other, 'c', [(0, 1), (1, 0)])  2.26 us
    unnamed x10, local copies, waits for them, and re-layouts  2.21 us
  transfers between devices with their start and end apart: 2, of which 2 were waited for; matrix products, arithmetic and copies ran while one was open for 0% of the time, Pallas kernels for 0%

profile of v1, /device:TPU:1, one launch (start us, length us, event | category | flops | bytes accessed | tf_op | source)
XLA Modules:
  0.0 96.9 jit_solution(13510763655861638758)
XLA Ops:
  0.0 0.0 copy-start
  0.0 0.0 copy-start.3
  0.0 0.0 copy-start.2
  0.0 0.9 reshape.55
  0.9 29.6 %all_to_all.20 = bf16[4,128,256]{2,1,0:T(8,128)(2,1)S(1)} all-to-all(bf16[4,128,256]{2,1,0:T(8,128)(2,1)S(1)} %reshape.55), channel_id=1, replica_groups=mesh['x'=4,'zl'=4,'c'=2,'zh'=4,'y'=4] {'zh'}, dimensions={0} | all-to-all | bytes 524288 | tf_op jit(solution)/shard_map/all_to_all | solution.py:73
  30.5 1.1 %broadcast_in_dim.2 = bf16[4,4,128,256]{3,2,1,0:T(8,128)(2,1)} broadcast(bf16[4,128,256]{2,1,0:T(8,128)(2,1)S(1)} %all_to_all.20), dimensions={1,2,3} | broadcast | bytes 1310720 | tf_op jit(solution)/shard_map/broadcast_in_dim | solution.py:71
  31.6 4.2 %all-to-all-start.1 = ((bf16[16,128,256]{2,1,0:T(8,128)(2,1)}), bf16[16,128,256]{2,1,0:T(8,128)(2,1)S(1)}, u32[]{:S(2)}, u32[]{:S(2)}) async-start(bf16[16,128,256]{2,1,0:T(8,128)(2,1)} %bitcast.1), calls=%async_computation.1 | async-start | bytes 2097152 | tf_op jit(solution)/shard_map/all_to_all | solution.py:73
  35.8 9.7 %all-to-all-done.1.feat_ref = bf16[16,128,256]{2,1,0:T(8,128)(2,1)S(1)} async-done(((bf16[16,128,256]{2,1,0:T(8,128)(2,1)}), bf16[16,128,256]{2,1,0:T(8,128)(2,1)S(1)}, u32[]{:S(2)}, u32[]{:S(2)}) %all-to-all-start.1) | async-done | bytes 1048608 | tf_op jit(solution)/shard_map/all_to_all | solution.py:73
  45.5 0.0 copy-done.3
  45.5 0.0 copy-done.2
  45.5 0.0 copy-start.1
  45.5 2.2 %copy-done.1 = bf16[128,128,128]{2,1,0:T(8,128)(2,1)S(1)} copy-done((bf16[128,128,128]{2,1,0:T(8,128)(2,1)S(1)}, bf16[128,128,128]{2,1,0:T(8,128)(2,1)}, u32[]{:S(2)}) %copy-start.1) | copy-done | bytes 4194328
  47.7 4.1 %tile_products.1 = (f32[16,128,256]{2,1,0:T(8,128)S(1)}, bf16[16,128,256]{2,1,0:T(8,128)(2,1)S(1)}) custom-call(s32[1]{0:T(128)} %bitcast.core_ref, s32[128]{0:T(128)S(1)} %copy-done.2, s32[128]{0:T(128)S(1)} %copy-done.3, bf16[128,128,128]{2,1,0:T(8,128)(2,1)S(1)} %copy-done.1, bf16[16,128,256]{2,1,0:T(8,128)(2,1)S(1)} %all-to-all-done.1.feat_ref), custom_call_target="tpu_custom_call" | custom-call | flops 1073741824 | bytes 4194304 | tf_op jit(solution)/shard_map/tile_products/pallas_call | solution.py:43
  51.8 8.8 %collective-permute-start = (bf16[16,128,256]{2,1,0:T(8,128)(2,1)S(1)}, bf16[16,128,256]{2,1,0:T(8,128)(2,1)S(1)}, u32[]{:S(2)}, u32[]{:S(2)}) collective-permute-start(bf16[16,128,256]{2,1,0:T(8,128)(2,1)S(1)} %get-tuple-element.8), channel_id=1, source_target_pairs={{0,16},{16,0},{1,17},{17,1},{2,18},{18,2},{3,19},{19,3},{4,20},{20... | collective-permute-start | bytes 3145736 | tf_op jit(solution)/shard_map/ppermute | solution.py:92
  60.6 2.3 %collective-permute-done = bf16[16,128,256]{2,1,0:T(8,128)(2,1)S(1)} collective-permute-done((bf16[16,128,256]{2,1,0:T(8,128)(2,1)S(1)}, bf16[16,128,256]{2,1,0:T(8,128)(2,1)S(1)}, u32[]{:S(2)}, u32[]{:S(2)}) %collective-permute-start) | collective-permute-done | bytes 1048608 | tf_op jit(solution)/shard_map/ppermute | solution.py:92
  62.9 0.4 add_convert_fusion
  63.2 18.1 %all_to_all.21 = bf16[16,128,256]{2,1,0:T(8,128)(2,1)S(1)} all-to-all(bf16[16,128,256]{2,1,0:T(8,128)(2,1)S(1)} %add_convert_fusion), channel_id=1, replica_groups=mesh['x'=4,'zl'=4,'c'=2,'zh'=4,'y'=4] {'x'}, dimensions={0} | all-to-all | bytes 2097152 | tf_op jit(solution)/shard_map/all_to_all | solution.py:78
  81.3 0.2 convert_element_type.28
  81.5 0.0 copy-start.4
  81.5 0.1 fusion.2
  81.7 14.4 %all_to_all.22 = bf16[4,128,256]{2,1,0:T(8,128)(2,1)S(1)} all-to-all(bf16[4,128,256]{2,1,0:T(8,128)(2,1)S(1)} %fusion.2), channel_id=1, replica_groups=mesh['x'=4,'zl'=4,'c'=2,'zh'=4,'y'=4] {'zl'}, dimensions={0} | all-to-all | bytes 524288 | tf_op jit(solution)/shard_map/all_to_all | solution.py:78
  96.1 0.0 copy-done
  96.1 0.0 copy-done.4
  96.1 0.8 fusion.1
  (1 shorter events, 0.0 us)
Async XLA Ops:
  0.0 96.1 %copy-start = (bf16[256,256]{1,0:T(8,128)(2,1)S(1)}, bf16[256,256]{1,0:T(8,128)(2,1)}, u32[]{:S(2)}) copy-start(bf16[256,256]{1,0:T(8,128)(2,1)} %param.10) | copy-start | bytes 393220
  0.0 45.5 %copy-start.3 = (s32[128]{0:T(128)S(1)}, s32[128]{0:T(128)}, u32[]{:S(2)}) copy-start(s32[128]{0:T(128)} %cols_ref.1) | copy-start | bytes 1540
  0.0 45.5 %copy-start.2 = (s32[128]{0:T(128)S(1)}, s32[128]{0:T(128)}, u32[]{:S(2)}) copy-start(s32[128]{0:T(128)} %rows_ref.1) | copy-start | bytes 1540
  31.6 13.9 %all-to-all-start.1 = ((bf16[16,128,256]{2,1,0:T(8,128)(2,1)}), bf16[16,128,256]{2,1,0:T(8,128)(2,1)S(1)}, u32[]{:S(2)}, u32[]{:S(2)}) async-start(bf16[16,128,256]{2,1,0:T(8,128)(2,1)} %bitcast.1), calls=%async_computation.1 | async-start | bytes 2097152 | tf_op jit(solution)/shard_map/all_to_all | solution.py:73
  45.5 2.2 %copy-start.1 = (bf16[128,128,128]{2,1,0:T(8,128)(2,1)S(1)}, bf16[128,128,128]{2,1,0:T(8,128)(2,1)}, u32[]{:S(2)}) copy-start(bf16[128,128,128]{2,1,0:T(8,128)(2,1)} %adj_ref.1) | copy-start | bytes 12582916
  51.8 11.1 %collective-permute-start = (bf16[16,128,256]{2,1,0:T(8,128)(2,1)S(1)}, bf16[16,128,256]{2,1,0:T(8,128)(2,1)S(1)}, u32[]{:S(2)}, u32[]{:S(2)}) collective-permute-start(bf16[16,128,256]{2,1,0:T(8,128)(2,1)S(1)} %get-tuple-element.8), channel_id=1, source_target_pairs={{0,16},{16,0},{1,17},{17,1},{2,18},{18,2},{3,19},{19,3},{4,20},{20... | collective-permute-start | bytes 3145736 | tf_op jit(solution)/shard_map/ppermute | solution.py:92
  81.5 14.6 %copy-start.4 = (f32[256]{0:T(256)S(1)}, f32[256]{0:T(256)}, u32[]{:S(2)}) copy-start(f32[256]{0:T(256)} %param.11) | copy-start | bytes 3076

commit v2 on v1

v2 whole, which is shorter than its diff:
```python
import functools

import jax
import jax.numpy as jnp
from jax import lax
from jax.experimental import pallas as pl
from jax.experimental.pallas import tpu as pltpu
from jax.sharding import Mesh, PartitionSpec as P

F32 = jnp.float32
BF16 = jnp.bfloat16
GROUP = 32
VMEM_LIMIT = 20 << 20


def tile_kernel(
    place_ref, rows_ref, cols_ref, adj_hbm, f0, f1, f2, f3, own_ref, other_ref, acc, feat, adj, sems
):
    half = own_ref.shape[0]
    count = adj.shape[0]
    groups = count // GROUP
    x = place_ref[0]
    core = place_ref[1]
    y = place_ref[2]

    def fetch(g):
        part = pl.ds(g * GROUP, GROUP)
        return pltpu.make_async_copy(adj_hbm.at[part], adj.at[part], sems.at[g])

    for g in range(groups):
        fetch(g).start()
    acc[...] = jnp.zeros_like(acc)
    for i, part in enumerate((f0, f1, f2, f3)):
        feat[4 * i : 4 * i + 4] = part[...]

    @pl.loop(0, groups)
    def _(g):
        fetch(g).wait()
        for k in range(GROUP):
            t = g * GROUP + k
            row = rows_ref[t]
            col = cols_ref[t]
            slot = ((row & 1) ^ core) * half + (((row >> 3) - x) & 3) * 4 + ((row >> 1) & 3)
            block = ((y - col) & 3) * 4 + (col >> 2)
            acc[slot] += jnp.dot(adj[t], feat[block], preferred_element_type=F32)

    own_ref[...] = acc[:half]
    other_ref[...] = acc[half:].astype(BF16)


def tile_products(place, rows, cols, tiles, parts):
    count, side, _ = tiles.shape
    width = parts[0].shape[2]
    half = 16
    vmem = pl.BlockSpec(memory_space=pltpu.VMEM)
    smem = pl.BlockSpec(memory_space=pltpu.SMEM)
    return pl.pallas_call(
        tile_kernel,
        out_shape=(
            jax.ShapeDtypeStruct((half, side, width), F32),
            jax.ShapeDtypeStruct((half, side, width), BF16),
        ),
        in_specs=[smem] * 3 + [pl.BlockSpec(memory_space=pltpu.HBM)] + [vmem] * 4,
        out_specs=(vmem, vmem),
        scratch_shapes=[
            pltpu.VMEM((2 * half, side, width), F32),
            pltpu.VMEM((16, side, width), BF16),
            pltpu.VMEM((count, side, side), BF16),
            pltpu.SemaphoreType.DMA((count // GROUP,)),
        ],
        cost_estimate=pl.CostEstimate(
            flops=2 * count * side * side * width,
            bytes_accessed=tiles.size * 2,
            transcendentals=0,
        ),
        compiler_params=pltpu.CompilerParams(vmem_limit_bytes=VMEM_LIMIT),
        name="tile_products",
    )(place, rows, cols, tiles, *parts)


def send(value, axis, distance):
    n = lax.axis_size(axis)
    return lax.ppermute(value, axis, [(i, (i + distance) % n) for i in range(n)])


def on_device(adjacency_tiles, row_block, column_block, features, weight, out_bias):
    place = jnp.stack([lax.axis_index(a) for a in ("x", "c", "y")]).astype(jnp.int32)
    column = lax.all_gather(features, "zh", axis=0)
    parts = [column] + [send(column, "y", d) for d in (1, 2, 3)]
    own, other = tile_products(place, row_block, column_block, adjacency_tiles, parts)
    received = send(other, "c", 1)
    chip = own + received.astype(F32)
    n = 4
    leaving = [chip[n * d : n * d + n].astype(BF16) for d in (1, 2, 3)]
    plane = chip[:n]
    for d in (1, 2, 3):
        plane = plane + send(leaving[d - 1], "x", d).astype(F32)
    zl = lax.axis_index("zl")
    arrived = lax.all_to_all(plane.astype(BF16), "zl", 0, 0, tiled=True).astype(F32)
    total = lax.optimization_barrier(lax.dynamic_index_in_dim(plane, zl, keepdims=False))
    for i in range(n):
        total = total + jnp.where(zl == i, 0.0, arrived[i])
    aggregate = total.astype(BF16)
    mixed = jnp.dot(aggregate, weight, preferred_element_type=F32) + out_bias
    return jax.nn.relu(mixed).astype(BF16)


def solution(mesh):
    fine = Mesh(mesh.devices.reshape(4, 4, 2, 4, 4), ("x", "zl", "c", "zh", "y"))
    every = ("x", "zl", "c", "zh", "y")
    in_specs = (P(every, None, None), P(every), P(every), P(every, None), P(), P())
    return jax.shard_map(
        on_device, mesh=fine, in_specs=in_specs, out_specs=P(every, None), check_vma=False
    )
```

time: 98.7 us -> 93.3 us (0.945)
  the two profiles are of different devices: /device:TPU:1 before, /device:TPU:2 now
where the time goes in v2:
time: 93.3 us; the launch traced here: 92.8 us
  waiting for transfers between devices  28.1 us (30%)
  starting transfers between devices  27.3 us (29%)
  blocking collectives  27.2 us (29%)
  Pallas kernels  4.3 us (5%)
  local copies, waits for them, and re-layouts  3.58 us (4%)
  other arithmetic  1.3 us (1%)
    all_gather x1, blocking collectives, on_device(): column = lax.all_gather(features, 'zh', axis=0)  27.2 us
    ppermute x7, starting transfers between devices, send(): lax.ppermute(value, axis, [(i, (i + distance) % n) for i in range(n)])  23.9 us
    ppermute x7, waiting for transfers between devices, send(): lax.ppermute(value, axis, [(i, (i + distance) % n) for i in range(n)])  18.8 us
    all_to_all x1, waiting for transfers between devices, on_device(): lax.all_to_all(plane.astype(BF16), 'zl', 0, 0, tiled=True).astype(F32)  9.26 us
    pallas_call x1, Pallas kernels, tile_products(): pl.pallas_call(tile_kernel, out_shape=(jax.ShapeDtypeStruct((half, side,...  4.3 us
    unnamed x10, local copies, waits for them, and re-layouts  3.51 us
    all_to_all x1, starting transfers between devices, on_device(): lax.all_to_all(plane.astype(BF16), 'zl', 0, 0, tiled=True).astype(F32)  3.4 us
  transfers between devices with their start and end apart: 8, of which 8 were waited for; matrix products, arithmetic and copies ran while one was open for 0% of the time, Pallas kernels for 0%

profile of v2, /device:TPU:2, one launch (start us, length us, event | category | flops | bytes accessed | tf_op | source)
XLA Modules:
  0.0 92.8 jit_solution(14698616832785060550)
XLA Ops:
  0.0 0.0 copy-start
  0.0 27.2 %all-gather = bf16[512,256]{1,0:T(8,128)(2,1)S(1)} all-gather(bf16[128,256]{1,0:T(8,128)(2,1)} %param.9), channel_id=2, replica_groups=mesh['x'=4,'zl'=4,'c'=2,'zh'=4,'y'=4] {'zh'}, dimensions={0}, use_global_device_ids=true | all-gather | bytes 327680 | tf_op jit(solution)/shard_map/all_gather | solution.py:88
  27.2 3.5 %collective-permute-start = (bf16[4,128,256]{2,1,0:T(8,128)(2,1)S(1)}, bf16[4,128,256]{2,1,0:T(8,128)(2,1)S(1)}, u32[]{:S(2)}, u32[]{:S(2)}) collective-permute-start(bf16[4,128,256]{2,1,0:T(8,128)(2,1)S(1)} %bitcast.35), channel_id=1, source_target_pairs={{0,1},{1,2},{2,3},{3,0},{4,5},{5,6},{6,7},{7,4},{8,9},{9,10},{10,1... | collective-permute-start | bytes 786440 | tf_op jit(solution)/shard_map/ppermute | solution.py:83
  30.7 4.8 %collective-permute-start.1 = (bf16[4,128,256]{2,1,0:T(8,128)(2,1)S(1)}, bf16[4,128,256]{2,1,0:T(8,128)(2,1)S(1)}, u32[]{:S(2)}, u32[]{:S(2)}) collective-permute-start(bf16[4,128,256]{2,1,0:T(8,128)(2,1)S(1)} %bitcast.36), channel_id=1, source_target_pairs={{0,2},{1,3},{2,0},{3,1},{4,6},{5,7},{6,4},{7,5},{8,10},{9,11},{10,... | collective-permute-start | bytes 786440 | tf_op jit(solution)/shard_map/ppermute | solution.py:83
  35.5 3.3 %collective-permute-start.2 = (bf16[4,128,256]{2,1,0:T(8,128)(2,1)S(1)}, bf16[4,128,256]{2,1,0:T(8,128)(2,1)S(1)}, u32[]{:S(2)}, u32[]{:S(2)}) collective-permute-start(bf16[4,128,256]{2,1,0:T(8,128)(2,1)S(1)} %bitcast.37), channel_id=1, source_target_pairs={{0,3},{1,0},{2,1},{3,2},{4,7},{5,4},{6,5},{7,6},{8,11},{9,8},{10,9... | collective-permute-start | bytes 786440 | tf_op jit(solution)/shard_map/ppermute | solution.py:83
  38.8 0.1 pad_add_fusion.place_ref
  38.9 0.6 collective-permute-done.f1
  39.5 3.2 %collective-permute-done.1.f2 = bf16[4,128,256]{2,1,0:T(8,128)(2,1)S(1)} collective-permute-done((bf16[4,128,256]{2,1,0:T(8,128)(2,1)S(1)}, bf16[4,128,256]{2,1,0:T(8,128)(2,1)S(1)}, u32[]{:S(2)}, u32[]{:S(2)}) %collective-permute-start.1) | collective-permute-done | bytes 262176 | tf_op jit(solution)/shard_map/ppermute | solution.py:83
  42.8 2.3 %collective-permute-done.2.f3 = bf16[4,128,256]{2,1,0:T(8,128)(2,1)S(1)} collective-permute-done((bf16[4,128,256]{2,1,0:T(8,128)(2,1)S(1)}, bf16[4,128,256]{2,1,0:T(8,128)(2,1)S(1)}, u32[]{:S(2)}, u32[]{:S(2)}) %collective-permute-start.2) | collective-permute-done | bytes 262176 | tf_op jit(solution)/shard_map/ppermute | solution.py:83
  45.1 0.0 copy-start.1
  45.1 2.2 %copy-done.1 = bf16[128,128,128]{2,1,0:T(8,128)(2,1)S(1)} copy-done((bf16[128,128,128]{2,1,0:T(8,128)(2,1)S(1)}, bf16[128,128,128]{2,1,0:T(8,128)(2,1)}, u32[]{:S(2)}) %copy-start.1) | copy-done | bytes 4194328
  47.3 0.0 copy-start.2
  47.3 0.7 copy-done.2
  47.9 0.0 copy-start.3
  47.9 0.7 copy-done.3
  48.6 4.3 %tile_products.1 = (f32[16,128,256]{2,1,0:T(8,128)S(1)}, bf16[16,128,256]{2,1,0:T(8,128)(2,1)S(1)}) custom-call(s32[3]{0:T(128)S(1)} %pad_add_fusion.place_ref, s32[128]{0:T(128)S(1)} %copy-done.2, s32[128]{0:T(128)S(1)} %copy-done.3, bf16[128,128,128]{2,1,0:T(8,128)(2,1)S(1)} %copy-done.1, bf16[4,128,256]{2,1,0:T(8,128)(2,1)S(1)} %bitcast.38, ...), custom_call_target="tpu_custom_call" | custom-call | flops 1073741824 | bytes 4194304 | tf_op jit(solution)/shard_map/tile_products/pallas_call | solution.py:57
  52.9 1.9 %collective-permute-start.3 = (bf16[16,128,256]{2,1,0:T(8,128)(2,1)S(1)}, bf16[16,128,256]{2,1,0:T(8,128)(2,1)S(1)}, u32[]{:S(2)}, u32[]{:S(2)}) collective-permute-start(bf16[16,128,256]{2,1,0:T(8,128)(2,1)S(1)} %get-tuple-element.8), channel_id=1, source_target_pairs={{0,16},{16,0},{1,17},{17,1},{2,18},{18,2},{3,19},{19,3},{4,20},{20... | collective-permute-start | bytes 3145736 | tf_op jit(solution)/shard_map/ppermute | solution.py:83
  54.8 2.6 %collective-permute-done.3 = bf16[16,128,256]{2,1,0:T(8,128)(2,1)S(1)} collective-permute-done((bf16[16,128,256]{2,1,0:T(8,128)(2,1)S(1)}, bf16[16,128,256]{2,1,0:T(8,128)(2,1)S(1)}, u32[]{:S(2)}, u32[]{:S(2)}) %collective-permute-start.3) | collective-permute-done | bytes 1048608 | tf_op jit(solution)/shard_map/ppermute | solution.py:83
  57.5 0.3 fusion.22
  57.8 0.1 fusion.23
  57.9 0.0 copy-start.4
  57.9 3.4 %collective-permute-start.4 = (bf16[4,128,256]{2,1,0:T(8,128)(2,1)S(1)}, bf16[4,128,256]{2,1,0:T(8,128)(2,1)S(1)}, u32[]{:S(2)}, u32[]{:S(2)}) collective-permute-start(bf16[4,128,256]{2,1,0:T(8,128)(2,1)S(1)} %get-tuple-element.13), channel_id=1, source_target_pairs={{0,128},{128,256},{256,384},{384,0},{1,129},{129,257},{257,385},{3... | collective-permute-start | bytes 786440 | tf_op jit(solution)/shard_map/ppermute | solution.py:83
  61.3 3.0 %collective-permute-start.5 = (bf16[4,128,256]{2,1,0:T(8,128)(2,1)S(1)}, bf16[4,128,256]{2,1,0:T(8,128)(2,1)S(1)}, u32[]{:S(2)}, u32[]{:S(2)}) collective-permute-start(bf16[4,128,256]{2,1,0:T(8,128)(2,1)S(1)} %get-tuple-element.15), channel_id=1, source_target_pairs={{0,256},{128,384},{256,0},{384,128},{1,257},{129,385},{257,1},{385... | collective-permute-start | bytes 786440 | tf_op jit(solution)/shard_map/ppermute | solution.py:83
  64.3 4.1 %collective-permute-start.6 = (bf16[4,128,256]{2,1,0:T(8,128)(2,1)S(1)}, bf16[4,128,256]{2,1,0:T(8,128)(2,1)S(1)}, u32[]{:S(2)}, u32[]{:S(2)}) collective-permute-start(bf16[4,128,256]{2,1,0:T(8,128)(2,1)S(1)} %get-tuple-element.14), channel_id=1, source_target_pairs={{0,384},{128,0},{256,128},{384,256},{1,385},{129,1},{257,129},{385... | collective-permute-start | bytes 786440 | tf_op jit(solution)/shard_map/ppermute | solution.py:83
  68.4 0.6 collective-permute-done.4
  69.0 5.0 %collective-permute-done.5 = bf16[4,128,256]{2,1,0:T(8,128)(2,1)S(1)} collective-permute-done((bf16[4,128,256]{2,1,0:T(8,128)(2,1)S(1)}, bf16[4,128,256]{2,1,0:T(8,128)(2,1)S(1)}, u32[]{:S(2)}, u32[]{:S(2)}) %collective-permute-start.5) | collective-permute-done | bytes 262176 | tf_op jit(solution)/shard_map/ppermute | solution.py:83
  73.9 4.5 %collective-permute-done.6 = bf16[4,128,256]{2,1,0:T(8,128)(2,1)S(1)} collective-permute-done((bf16[4,128,256]{2,1,0:T(8,128)(2,1)S(1)}, bf16[4,128,256]{2,1,0:T(8,128)(2,1)S(1)}, u32[]{:S(2)}, u32[]{:S(2)}) %collective-permute-start.6) | collective-permute-done | bytes 262176 | tf_op jit(solution)/shard_map/ppermute | solution.py:83
  78.4 0.8 fusion.20
  79.2 3.4 %all-to-all-start = ((bf16[4,128,256]{2,1,0:T(8,128)(2,1)}), bf16[4,128,256]{2,1,0:T(8,128)(2,1)S(1)}, u32[]{:S(2)}, u32[]{:S(2)}) async-start(bf16[4,128,256]{2,1,0:T(8,128)(2,1)} %get-tuple-element.9), calls=%async_computation | async-start | bytes 524288 | tf_op jit(solution)/shard_map/all_to_all | solution.py:99
  82.7 9.3 %all-to-all-done = bf16[4,128,256]{2,1,0:T(8,128)(2,1)S(1)} async-done(((bf16[4,128,256]{2,1,0:T(8,128)(2,1)}), bf16[4,128,256]{2,1,0:T(8,128)(2,1)S(1)}, u32[]{:S(2)}, u32[]{:S(2)}) %all-to-all-start) | async-done | bytes 262176 | tf_op jit(solution)/shard_map/all_to_all | solution.py:99
  92.0 0.0 copy-done
  92.0 0.0 copy-done.4
  92.0 0.8 fusion.1
  (2 shorter events, 0.1 us)
Async XLA Ops:
  0.0 92.0 %copy-start = (bf16[256,256]{1,0:T(8,128)(2,1)S(1)}, bf16[256,256]{1,0:T(8,128)(2,1)}, u32[]{:S(2)}) copy-start(bf16[256,256]{1,0:T(8,128)(2,1)} %param.10) | copy-start | bytes 393220
  27.2 12.3 %collective-permute-start = (bf16[4,128,256]{2,1,0:T(8,128)(2,1)S(1)}, bf16[4,128,256]{2,1,0:T(8,128)(2,1)S(1)}, u32[]{:S(2)}, u32[]{:S(2)}) collective-permute-start(bf16[4,128,256]{2,1,0:T(8,128)(2,1)S(1)} %bitcast.35), channel_id=1, source_target_pairs={{0,1},{1,2},{2,3},{3,0},{4,5},{5,6},{6,7},{7,4},{8,9},{9,10},{10,1... | collective-permute-start | bytes 786440 | tf_op jit(solution)/shard_map/ppermute | solution.py:83
  30.7 12.0 %collective-permute-start.1 = (bf16[4,128,256]{2,1,0:T(8,128)(2,1)S(1)}, bf16[4,128,256]{2,1,0:T(8,128)(2,1)S(1)}, u32[]{:S(2)}, u32[]{:S(2)}) collective-permute-start(bf16[4,128,256]{2,1,0:T(8,128)(2,1)S(1)} %bitcast.36), channel_id=1, source_target_pairs={{0,2},{1,3},{2,0},{3,1},{4,6},{5,7},{6,4},{7,5},{8,10},{9,11},{10,... | collective-permute-start | bytes 786440 | tf_op jit(solution)/shard_map/ppermute | solution.py:83
  35.5 9.6 %collective-permute-start.2 = (bf16[4,128,256]{2,1,0:T(8,128)(2,1)S(1)}, bf16[4,128,256]{2,1,0:T(8,128)(2,1)S(1)}, u32[]{:S(2)}, u32[]{:S(2)}) collective-permute-start(bf16[4,128,256]{2,1,0:T(8,128)(2,1)S(1)} %bitcast.37), channel_id=1, source_target_pairs={{0,3},{1,0},{2,1},{3,2},{4,7},{5,4},{6,5},{7,6},{8,11},{9,8},{10,9... | collective-permute-start | bytes 786440 | tf_op jit(solution)/shard_map/ppermute | solution.py:83
  45.1 2.2 %copy-start.1 = (bf16[128,128,128]{2,1,0:T(8,128)(2,1)S(1)}, bf16[128,128,128]{2,1,0:T(8,128)(2,1)}, u32[]{:S(2)}) copy-start(bf16[128,128,128]{2,1,0:T(8,128)(2,1)} %adj_hbm.1) | copy-start | bytes 12582916
  47.3 0.7 copy-start.2
  47.9 0.7 copy-start.3
  52.9 4.6 %collective-permute-start.3 = (bf16[16,128,256]{2,1,0:T(8,128)(2,1)S(1)}, bf16[16,128,256]{2,1,0:T(8,128)(2,1)S(1)}, u32[]{:S(2)}, u32[]{:S(2)}) collective-permute-start(bf16[16,128,256]{2,1,0:T(8,128)(2,1)S(1)} %get-tuple-element.8), channel_id=1, source_target_pairs={{0,16},{16,0},{1,17},{17,1},{2,18},{18,2},{3,19},{19,3},{4,20},{20... | collective-permute-start | bytes 3145736 | tf_op jit(solution)/shard_map/ppermute | solution.py:83
  57.9 34.1 %copy-start.4 = (f32[256]{0:T(256)S(1)}, f32[256]{0:T(256)}, u32[]{:S(2)}) copy-start(f32[256]{0:T(256)} %param.11) | copy-start | bytes 3076
  57.9 11.1 %collective-permute-start.4 = (bf16[4,128,256]{2,1,0:T(8,128)(2,1)S(1)}, bf16[4,128,256]{2,1,0:T(8,128)(2,1)S(1)}, u32[]{:S(2)}, u32[]{:S(2)}) collective-permute-start(bf16[4,128,256]{2,1,0:T(8,128)(2,1)S(1)} %get-tuple-element.13), channel_id=1, source_target_pairs={{0,128},{128,256},{256,384},{384,0},{1,129},{129,257},{257,385},{3... | collective-permute-start | bytes 786440 | tf_op jit(solution)/shard_map/ppermute | solution.py:83
  61.3 12.6 %collective-permute-start.5 = (bf16[4,128,256]{2,1,0:T(8,128)(2,1)S(1)}, bf16[4,128,256]{2,1,0:T(8,128)(2,1)S(1)}, u32[]{:S(2)}, u32[]{:S(2)}) collective-permute-start(bf16[4,128,256]{2,1,0:T(8,128)(2,1)S(1)} %get-tuple-element.15), channel_id=1, source_target_pairs={{0,256},{128,384},{256,0},{384,128},{1,257},{129,385},{257,1},{385... | collective-permute-start | bytes 786440 | tf_op jit(solution)/shard_map/ppermute | solution.py:83
  64.3 14.1 %collective-permute-start.6 = (bf16[4,128,256]{2,1,0:T(8,128)(2,1)S(1)}, bf16[4,128,256]{2,1,0:T(8,128)(2,1)S(1)}, u32[]{:S(2)}, u32[]{:S(2)}) collective-permute-start(bf16[4,128,256]{2,1,0:T(8,128)(2,1)S(1)} %get-tuple-element.14), channel_id=1, source_target_pairs={{0,384},{128,0},{256,128},{384,256},{1,385},{129,1},{257,129},{385... | collective-permute-start | bytes 786440 | tf_op jit(solution)/shard_map/ppermute | solution.py:83
  79.2 12.7 %all-to-all-start = ((bf16[4,128,256]{2,1,0:T(8,128)(2,1)}), bf16[4,128,256]{2,1,0:T(8,128)(2,1)S(1)}, u32[]{:S(2)}, u32[]{:S(2)}) async-start(bf16[4,128,256]{2,1,0:T(8,128)(2,1)} %get-tuple-element.9), calls=%async_computation | async-start | bytes 524288 | tf_op jit(solution)/shard_map/all_to_all | solution.py:99

commit v3 on v2

v3 whole, which is shorter than its diff:
```python
import jax
import jax.numpy as jnp
from jax import lax
from jax.experimental import pallas as pl
from jax.experimental.pallas import tpu as pltpu
from jax.sharding import Mesh, PartitionSpec as P

F32 = jnp.float32
BF16 = jnp.bfloat16
GROUP = 32
VMEM_LIMIT = 50 << 20


def tile_kernel(
    core_ref, rows_ref, cols_ref, adj_hbm, feat, own_ref, other_ref, acc, adj, sems
):
    half = own_ref.shape[0]
    count = adj.shape[0]
    groups = count // GROUP
    core = core_ref[0]

    def fetch(g):
        part = pl.ds(g * GROUP, GROUP)
        return pltpu.make_async_copy(adj_hbm.at[part], adj.at[part], sems.at[g])

    for g in range(groups):
        fetch(g).start()
    acc[...] = jnp.zeros_like(acc)

    @pl.loop(0, groups)
    def _(g):
        fetch(g).wait()
        for k in range(GROUP):
            t = g * GROUP + k
            row = rows_ref[t]
            col = cols_ref[t]
            slot = ((row & 1) ^ core) * half + (row >> 1)
            block = (col & 3) * 4 + (col >> 2)
            acc[slot] += jnp.dot(adj[t], feat[block], preferred_element_type=F32)

    own_ref[...] = acc[:half]
    other_ref[...] = acc[half:].astype(BF16)


def tile_products(core, rows, cols, tiles, section):
    count, side, _ = tiles.shape
    width = section.shape[2]
    half = 16
    vmem = pl.BlockSpec(memory_space=pltpu.VMEM)
    smem = pl.BlockSpec(memory_space=pltpu.SMEM)
    return pl.pallas_call(
        tile_kernel,
        out_shape=(
            jax.ShapeDtypeStruct((half, side, width), F32),
            jax.ShapeDtypeStruct((half, side, width), BF16),
        ),
        in_specs=[smem] * 3 + [pl.BlockSpec(memory_space=pltpu.HBM)] + [vmem],
        out_specs=(vmem, vmem),
        scratch_shapes=[
            pltpu.VMEM((2 * half, side, width), F32),
            pltpu.VMEM((count, side, side), BF16),
            pltpu.SemaphoreType.DMA((count // GROUP,)),
        ],
        cost_estimate=pl.CostEstimate(
            flops=2 * count * side * side * width,
            bytes_accessed=tiles.size * 2,
            transcendentals=0,
        ),
        compiler_params=pltpu.CompilerParams(vmem_limit_bytes=VMEM_LIMIT),
        name="tile_products",
    )(core, rows, cols, tiles, section)


def sum_scatter(blocks, axis):
    n = lax.axis_size(axis)
    me = lax.axis_index(axis)
    share = blocks.shape[0] // n
    arrived = lax.all_to_all(blocks.astype(BF16), axis, 0, 0, tiled=True).astype(F32)
    total = lax.optimization_barrier(lax.dynamic_slice_in_dim(blocks, me * share, share))
    for i in range(n):
        total = total + jnp.where(me == i, 0.0, arrived[i * share : (i + 1) * share])
    return total


def on_device(adjacency_tiles, row_block, column_block, features, weight, out_bias):
    core = lax.axis_index("c").reshape(1).astype(jnp.int32)
    column = lax.all_gather(features, "zh", axis=0)
    copies = jnp.broadcast_to(column[None], (4,) + column.shape).reshape(-1, *column.shape[1:])
    section = lax.all_to_all(copies, "y", 0, 0, tiled=True)
    own, other = tile_products(core, row_block, column_block, adjacency_tiles, section)
    received = lax.ppermute(other, "c", [(0, 1), (1, 0)])
    chip = own + received.astype(F32)
    plane = sum_scatter(chip, "x")
    aggregate = sum_scatter(plane, "zl")[0].astype(BF16)
    mixed = jnp.dot(aggregate, weight, preferred_element_type=F32) + out_bias
    return jax.nn.relu(mixed).astype(BF16)


def solution(mesh):
    fine = Mesh(mesh.devices.reshape(4, 4, 2, 4, 4), ("x", "zl", "c", "zh", "y"))
    every = ("x", "zl", "c", "zh", "y")
    in_specs = (P(every, None, None), P(every), P(every), P(every, None), P(), P())
    return jax.shard_map(
        on_device, mesh=fine, in_specs=in_specs, out_specs=P(every, None), check_vma=False
    )
```

time: 93.3 us -> 91.9 us (0.985)
  starting transfers between devices: 27.3 us -> 14.6 us
  waiting for transfers between devices: 28.1 us -> 36.6 us
  other arithmetic: 1.3 us -> 4.07 us
  Pallas kernels: 4.3 us -> 6.12 us
  local copies, waits for them, and re-layouts: 3.58 us -> 1.95 us
    all_to_all x1 -> x3, waiting for transfers between devices: 9.26 us -> 34 us  [the longest x2 21.4 us: sum_scatter(): lax.all_to_all(blocks.astype(BF16), axis, 0, 0, tiled=True).astype(F32)]
    ppermute x7 -> x1, starting transfers between devices: 23.9 us -> 1.92 us  [on_device(): received = lax.ppermute(other, 'c', [(0, 1), (1, 0)])]
    ppermute x7 -> x1, waiting for transfers between devices: 18.8 us -> 2.63 us  [on_device(): received = lax.ppermute(other, 'c', [(0, 1), (1, 0)])]
    all_to_all x1 -> x3, starting transfers between devices: 3.4 us -> 12.7 us  [the longest x2 8.24 us: sum_scatter(): lax.all_to_all(blocks.astype(BF16), axis, 0, 0, tiled=True).astype(F32)]
    unnamed x10, local copies, waits for them, and re-layouts: 3.51 us -> 0.02 us
    convert_element_type x2 -> x4, other arithmetic: 0.88 us -> 4.07 us  [the longest x2 3.81 us: sum_scatter(): blocks.astype(BF16)]
    pallas_call x1, Pallas kernels: 4.3 us -> 6.12 us  [tile_products(): pl.pallas_call(tile_kernel, out_shape=(jax.ShapeDtypeStruct((half, side,...]
    broadcast_in_dim x0 -> x1, local copies, waits for them, and re-layouts: none -> 1.09 us  [on_device(): jnp.broadcast_to(column[None], (4,) + column.shape)]
  transfers between devices with their start and end apart: 8 -> 4, of which waited for: 8 -> 4; matrix products, arithmetic and copies ran while one was open for 0% -> 1% of each run, Pallas kernels for 0% -> 0%
where the time goes in v3:
time: 91.9 us; the launch traced here: 91.5 us
  waiting for transfers between devices  36.6 us (40%)
  blocking collectives  27.2 us (30%)
  starting transfers between devices  14.6 us (16%)
  Pallas kernels  6.12 us (7%)
  other arithmetic  4.07 us (4%)
  local copies, waits for them, and re-layouts  1.95 us (2%)
    all_gather x1, blocking collectives, on_device(): column = lax.all_gather(features, 'zh', axis=0)  27.2 us
    all_to_all x2, waiting for transfers between devices, sum_scatter(): lax.all_to_all(blocks.astype(BF16), axis, 0, 0, tiled=True).astype(F32)  21.4 us
    all_to_all x1, waiting for transfers between devices, on_device(): section = lax.all_to_all(copies, 'y', 0, 0, tiled=True)  12.6 us
    all_to_all x2, starting transfers between devices, sum_scatter(): lax.all_to_all(blocks.astype(BF16), axis, 0, 0, tiled=True).astype(F32)  8.24 us
    pallas_call x1, Pallas kernels, tile_products(): pl.pallas_call(tile_kernel, out_shape=(jax.ShapeDtypeStruct((half, side,...  6.12 us
    all_to_all x1, starting transfers between devices, on_device(): section = lax.all_to_all(copies, 'y', 0, 0, tiled=True)  4.46 us
    convert_element_type x2, other arithmetic, sum_scatter(): blocks.astype(BF16)  3.81 us
    ppermute x1, waiting for transfers between devices, on_device(): received = lax.ppermute(other, 'c', [(0, 1), (1, 0)])  2.63 us
  transfers between devices with their start and end apart: 4, of which 4 were waited for; matrix products, arithmetic and copies ran while one was open for 1% of the time, Pallas kernels for 0%

profile of v3, /device:TPU:2, one launch (start us, length us, event | category | flops | bytes accessed | tf_op | source)
XLA Modules:
  0.0 91.5 jit_solution(788332707305189565)
XLA Ops:
  0.0 0.0 copy-start
  0.0 0.0 copy-start.1
  0.0 0.0 copy-start.2
  0.0 27.2 %all-gather = bf16[512,256]{1,0:T(8,128)(2,1)S(1)} all-gather(bf16[128,256]{1,0:T(8,128)(2,1)} %param.9), channel_id=2, replica_groups=mesh['x'=4,'zl'=4,'c'=2,'zh'=4,'y'=4] {'zh'}, dimensions={0}, use_global_device_ids=true | all-gather | bytes 327680 | tf_op jit(solution)/shard_map/all_gather | solution.py:87
  27.3 1.1 %broadcast_in_dim.21 = bf16[4,4,128,256]{3,2,1,0:T(8,128)(2,1)} broadcast(bf16[4,128,256]{2,1,0:T(8,128)(2,1)S(1)} %bitcast.7), dimensions={1,2,3} | broadcast | bytes 1310720 | tf_op jit(solution)/shard_map/broadcast_in_dim | solution.py:88
  28.3 4.5 %all-to-all-start = ((bf16[16,128,256]{2,1,0:T(8,128)(2,1)}), bf16[16,128,256]{2,1,0:T(8,128)(2,1)S(1)}, u32[]{:S(2)}, u32[]{:S(2)}) async-start(bf16[16,128,256]{2,1,0:T(8,128)(2,1)} %bitcast.2), calls=%async_computation | async-start | bytes 2097152 | tf_op jit(solution)/shard_map/all_to_all | solution.py:89
  32.8 12.6 %all-to-all-done.feat = bf16[16,128,256]{2,1,0:T(8,128)(2,1)S(1)} async-done(((bf16[16,128,256]{2,1,0:T(8,128)(2,1)}), bf16[16,128,256]{2,1,0:T(8,128)(2,1)S(1)}, u32[]{:S(2)}, u32[]{:S(2)}) %all-to-all-start) | async-done | bytes 1048608 | tf_op jit(solution)/shard_map/all_to_all | solution.py:89
  45.4 0.0 copy-done.1
  45.4 0.0 copy-done.2
  45.4 6.1 %tile_products.1 = (f32[16,128,256]{2,1,0:T(8,128)}, bf16[16,128,256]{2,1,0:T(8,128)(2,1)S(1)}) custom-call(s32[1]{0:T(128)} %bitcast.core_ref, s32[128]{0:T(128)S(1)} %copy-done.1, s32[128]{0:T(128)S(1)} %copy-done.2, bf16[128,128,128]{2,1,0:T(8,128)(2,1)} %adj_hbm.1, bf16[16,128,256]{2,1,0:T(8,128)(2,1)S(1)} %all-to-all-done.feat), custom_call_target="tpu_custom_call" | custom-call | flops 1073741824 | bytes 4194304 | tf_op jit(solution)/shard_map/tile_products/pallas_call | solution.py:51
  51.6 1.9 %collective-permute-start = (bf16[16,128,256]{2,1,0:T(8,128)(2,1)S(1)}, bf16[16,128,256]{2,1,0:T(8,128)(2,1)S(1)}, u32[]{:S(2)}, u32[]{:S(2)}) collective-permute-start(bf16[16,128,256]{2,1,0:T(8,128)(2,1)S(1)} %get-tuple-element.8), channel_id=1, source_target_pairs={{0,16},{16,0},{1,17},{17,1},{2,18},{18,2},{3,19},{19,3},{4,20},{20... | collective-permute-start | bytes 3145736 | tf_op jit(solution)/shard_map/ppermute | solution.py:91
  53.5 2.6 %collective-permute-done = bf16[16,128,256]{2,1,0:T(8,128)(2,1)S(1)} collective-permute-done((bf16[16,128,256]{2,1,0:T(8,128)(2,1)S(1)}, bf16[16,128,256]{2,1,0:T(8,128)(2,1)S(1)}, u32[]{:S(2)}, u32[]{:S(2)}) %collective-permute-start) | collective-permute-done | bytes 1048608 | tf_op jit(solution)/shard_map/ppermute | solution.py:91
  56.1 2.9 %fusion.20 = (bf16[16,128,256]{2,1,0:T(8,128)(2,1)}, f32[16,128,256]{2,1,0:T(8,128)S(1)}) fusion(f32[16,128,256]{2,1,0:T(8,128)} %get-tuple-element.7, bf16[16,128,256]{2,1,0:T(8,128)(2,1)S(1)} %collective-permute-done), kind=kLoop, calls=%fused_computation.30 | loop fusion | flops 1572864 | bytes 6291456 | tf_op jit(solution)/shard_map/convert_element_type | solution.py:78
  59.0 4.8 %all-to-all-start.1 = ((bf16[16,128,256]{2,1,0:T(8,128)(2,1)}), bf16[16,128,256]{2,1,0:T(8,128)(2,1)S(1)}, u32[]{:S(2)}, u32[]{:S(2)}) async-start(bf16[16,128,256]{2,1,0:T(8,128)(2,1)} %get-tuple-element.11), calls=%async_computation.1 | async-start | bytes 2097152 | tf_op jit(solution)/shard_map/all_to_all | solution.py:78
  63.9 0.8 constant_dynamic-slice_fusion.1
  64.7 0.0 copy-start.3
  64.7 13.1 %all-to-all-done.1 = bf16[16,128,256]{2,1,0:T(8,128)(2,1)S(1)} async-done(((bf16[16,128,256]{2,1,0:T(8,128)(2,1)}), bf16[16,128,256]{2,1,0:T(8,128)(2,1)S(1)}, u32[]{:S(2)}, u32[]{:S(2)}) %all-to-all-start.1) | async-done | bytes 1048608 | tf_op jit(solution)/shard_map/all_to_all | solution.py:78
  77.8 0.2 convert_element_type.26
  78.0 0.0 copy-done.3
  78.0 0.0 copy-start.4
  78.0 0.9 fusion.18
  79.0 3.4 %all-to-all-start.2 = ((bf16[4,128,256]{2,1,0:T(8,128)(2,1)}), bf16[4,128,256]{2,1,0:T(8,128)(2,1)S(1)}, u32[]{:S(2)}, u32[]{:S(2)}) async-start(bf16[4,128,256]{2,1,0:T(8,128)(2,1)} %get-tuple-element.9), calls=%async_computation.2 | async-start | bytes 524288 | tf_op jit(solution)/shard_map/all_to_all | solution.py:78
  82.4 8.2 %all-to-all-done.2 = bf16[4,128,256]{2,1,0:T(8,128)(2,1)S(1)} async-done(((bf16[4,128,256]{2,1,0:T(8,128)(2,1)}), bf16[4,128,256]{2,1,0:T(8,128)(2,1)S(1)}, u32[]{:S(2)}, u32[]{:S(2)}) %all-to-all-start.2) | async-done | bytes 262176 | tf_op jit(solution)/shard_map/all_to_all | solution.py:78
  90.7 0.0 copy-done
  90.7 0.0 copy-done.4
  90.7 0.8 fusion.1
  (2 shorter events, 0.1 us)
Async XLA Ops:
  0.0 90.7 %copy-start = (bf16[256,256]{1,0:T(8,128)(2,1)S(1)}, bf16[256,256]{1,0:T(8,128)(2,1)}, u32[]{:S(2)}) copy-start(bf16[256,256]{1,0:T(8,128)(2,1)} %param.10) | copy-start | bytes 393220
  0.0 45.4 %copy-start.1 = (s32[128]{0:T(128)S(1)}, s32[128]{0:T(128)}, u32[]{:S(2)}) copy-start(s32[128]{0:T(128)} %rows_ref.1) | copy-start | bytes 1540
  0.0 45.4 %copy-start.2 = (s32[128]{0:T(128)S(1)}, s32[128]{0:T(128)}, u32[]{:S(2)}) copy-start(s32[128]{0:T(128)} %cols_ref.1) | copy-start | bytes 1540
  28.3 17.1 %all-to-all-start = ((bf16[16,128,256]{2,1,0:T(8,128)(2,1)}), bf16[16,128,256]{2,1,0:T(8,128)(2,1)S(1)}, u32[]{:S(2)}, u32[]{:S(2)}) async-start(bf16[16,128,256]{2,1,0:T(8,128)(2,1)} %bitcast.2), calls=%async_computation | async-start | bytes 2097152 | tf_op jit(solution)/shard_map/all_to_all | solution.py:89
  51.6 4.6 %collective-permute-start = (bf16[16,128,256]{2,1,0:T(8,128)(2,1)S(1)}, bf16[16,128,256]{2,1,0:T(8,128)(2,1)S(1)}, u32[]{:S(2)}, u32[]{:S(2)}) collective-permute-start(bf16[16,128,256]{2,1,0:T(8,128)(2,1)S(1)} %get-tuple-element.8), channel_id=1, source_target_pairs={{0,16},{16,0},{1,17},{17,1},{2,18},{18,2},{3,19},{19,3},{4,20},{20... | collective-permute-start | bytes 3145736 | tf_op jit(solution)/shard_map/ppermute | solution.py:91
  59.0 18.8 %all-to-all-start.1 = ((bf16[16,128,256]{2,1,0:T(8,128)(2,1)}), bf16[16,128,256]{2,1,0:T(8,128)(2,1)S(1)}, u32[]{:S(2)}, u32[]{:S(2)}) async-start(bf16[16,128,256]{2,1,0:T(8,128)(2,1)} %get-tuple-element.11), calls=%async_computation.1 | async-start | bytes 2097152 | tf_op jit(solution)/shard_map/all_to_all | solution.py:78
  64.7 13.3 %copy-start.3 = (f32[4,128,256]{2,1,0:T(8,128)S(1)}, f32[4,128,256]{2,1,0:T(8,128)}, u32[]{:S(2)}) copy-start(f32[4,128,256]{2,1,0:T(8,128)} %constant_dynamic-slice_fusion.1) | copy-start | bytes 1572868
  78.0 12.7 %copy-start.4 = (f32[256]{0:T(256)S(1)}, f32[256]{0:T(256)}, u32[]{:S(2)}) copy-start(f32[256]{0:T(256)} %param.11) | copy-start | bytes 3076
  79.0 11.7 %all-to-all-start.2 = ((bf16[4,128,256]{2,1,0:T(8,128)(2,1)}), bf16[4,128,256]{2,1,0:T(8,128)(2,1)S(1)}, u32[]{:S(2)}, u32[]{:S(2)}) async-start(bf16[4,128,256]{2,1,0:T(8,128)(2,1)} %get-tuple-element.9), calls=%async_computation.2 | async-start | bytes 524288 | tf_op jit(solution)/shard_map/all_to_all | solution.py:78

commit v4 on v3

v4 whole, which is shorter than its diff:
```python
import jax
import jax.numpy as jnp
from jax import lax
from jax.experimental import pallas as pl
from jax.experimental.pallas import tpu as pltpu
from jax.sharding import Mesh, PartitionSpec as P

F32 = jnp.float32
BF16 = jnp.bfloat16
GROUP = 32
PIECE = 8
VMEM_LIMIT = 48 << 20


def tile_kernel(
    rows_ref, cols_ref, adj_hbm, feat, own_ref, other_ref, acc, adj, sems
):
    half = own_ref.shape[0]
    count = adj.shape[0]
    core = lax.axis_index("c")

    def fetch(i):
        part = pl.ds(i * PIECE, PIECE)
        return pltpu.make_async_copy(adj_hbm.at[part], adj.at[part], sems.at[i])

    for i in range(count // PIECE):
        fetch(i).start()
    acc[...] = jnp.zeros_like(acc)

    def run(first, size):
        for i in range(size // PIECE):
            fetch(first // PIECE + i).wait()
        for k in range(size):
            t = first + k
            row = rows_ref[t]
            col = cols_ref[t]
            to_x = row >> 3
            to_zl = (row >> 1) & 3
            chip = jnp.where((row & 1) == 0, 4 * to_x + to_zl, 4 * to_zl + to_x)
            slot = ((row & 1) ^ core) * half + chip
            block = (col & 3) * 4 + (col >> 2)
            acc[slot] += jnp.dot(adj[t], feat[block], preferred_element_type=F32)

    run(0, GROUP // 2)
    run(GROUP // 2, GROUP // 2)

    @pl.loop(1, count // GROUP)
    def _(g):
        run(g * GROUP, GROUP)

    own_ref[...] = acc[:half]
    other_ref[...] = acc[half:].astype(BF16)


def tile_products(rows, cols, tiles, section):
    count, side, _ = tiles.shape
    width = section.shape[2]
    half = 16
    vmem = pl.BlockSpec(memory_space=pltpu.VMEM)
    smem = pl.BlockSpec(memory_space=pltpu.SMEM)
    return pl.pallas_call(
        tile_kernel,
        out_shape=(
            jax.ShapeDtypeStruct((half, side, width), F32),
            jax.ShapeDtypeStruct((half, side, width), BF16),
        ),
        in_specs=[smem] * 2 + [pl.BlockSpec(memory_space=pltpu.HBM)] + [vmem],
        out_specs=(vmem, vmem),
        scratch_shapes=[
            pltpu.VMEM((2 * half, side, width), F32),
            pltpu.VMEM((count, side, side), BF16),
            pltpu.SemaphoreType.DMA((count // PIECE,)),
        ],
        cost_estimate=pl.CostEstimate(
            flops=2 * count * side * side * width,
            bytes_accessed=tiles.size * 2,
            transcendentals=0,
        ),
        compiler_params=pltpu.CompilerParams(vmem_limit_bytes=VMEM_LIMIT),
        name="tile_products",
    )(rows, cols, tiles, section)


def exchange(blocks, turned):
    along_x = [[(x * 4 + z) * 2 + turned for x in range(4)] for z in range(4)]
    along_zl = [[(x * 4 + z) * 2 + 1 - turned for z in range(4)] for x in range(4)]
    arrived = lax.all_to_all(
        blocks.astype(BF16),
        ("x", "zl", "c"),
        0,
        0,
        axis_index_groups=along_x + along_zl,
        tiled=True,
    )
    share = blocks.shape[0] // 4
    parts = arrived.astype(F32)
    total = parts[:share]
    for i in range(1, 4):
        total = total + parts[i * share : (i + 1) * share]
    return total


def on_device(adjacency_tiles, row_block, column_block, features, weight, out_bias):
    column = lax.all_gather(features, "zh", axis=0)
    copies = jnp.broadcast_to(column[None], (4,) + column.shape).reshape(-1, *column.shape[1:])
    section = lax.all_to_all(copies, "y", 0, 0, tiled=True)
    own, other = tile_products(row_block, column_block, adjacency_tiles, section)
    received = lax.ppermute(other, "c", [(0, 1), (1, 0)])
    chip = own + received.astype(F32)
    plane = exchange(chip, 0)
    aggregate = exchange(plane, 1)[0].astype(BF16)
    mixed = jnp.dot(aggregate, weight, preferred_element_type=F32) + out_bias
    return jax.nn.relu(mixed).astype(BF16)


def solution(mesh):
    fine = Mesh(mesh.devices.reshape(4, 4, 2, 4, 4), ("x", "zl", "c", "zh", "y"))
    every = ("x", "zl", "c", "zh", "y")
    in_specs = (P(every, None, None), P(every), P(every), P(every, None), P(), P())
    return jax.shard_map(
        on_device, mesh=fine, in_specs=in_specs, out_specs=P(every, None), check_vma=False
    )
```

time: 91.9 us -> 83.8 us (0.912)
  the two profiles are of different devices: /device:TPU:2 before, /device:TPU:1 now
where the time goes in v4:
time: 83.8 us; the launch traced here: 83.6 us
  blocking collectives  67.9 us (81%)
  starting transfers between devices  6.48 us (8%)
  Pallas kernels  5.26 us (6%)
  waiting for transfers between devices  2.26 us (3%)
    all_to_all x2, blocking collectives, exchange(): lax.all_to_all(blocks.astype(BF16), ('x', 'zl', 'c'), 0, 0, axis_index_gr...  26.8 us
    all_gather x1, blocking collectives, on_device(): column = lax.all_gather(features, 'zh', axis=0)  25.6 us
    all_to_all x1, blocking collectives, on_device(): section = lax.all_to_all(copies, 'y', 0, 0, tiled=True)  15.5 us
    ppermute x1, starting transfers between devices, on_device(): received = lax.ppermute(other, 'c', [(0, 1), (1, 0)])  6.48 us
    pallas_call x1, Pallas kernels, tile_products(): pl.pallas_call(tile_kernel, out_shape=(jax.ShapeDtypeStruct((half, side,...  5.26 us
    ppermute x1, waiting for transfers between devices, on_device(): received = lax.ppermute(other, 'c', [(0, 1), (1, 0)])  2.26 us
  transfers between devices with their start and end apart: 1, of which 1 were waited for; matrix products, arithmetic and copies ran while one was open for 0% of the time, Pallas kernels for 0%

profile of v4, /device:TPU:1, one launch (start us, length us, event | category | flops | bytes accessed | tf_op | source)
XLA Modules:
  0.0 83.6 jit_solution(15170487153217045636)
XLA Ops:
  0.0 0.0 copy-start
  0.0 0.0 copy-start.2
  0.0 0.0 copy-start.1
  0.0 25.6 %all-gather = bf16[512,256]{1,0:T(8,128)(2,1)S(1)} all-gather(bf16[128,256]{1,0:T(8,128)(2,1)} %param.9), channel_id=2, replica_groups=mesh['x'=4,'zl'=4,'c'=2,'zh'=4,'y'=4] {'zh'}, dimensions={0}, use_global_device_ids=true | all-gather | bytes 327680 | tf_op jit(solution)/shard_map/all_gather | solution.py:104
  25.6 0.1 broadcast_in_dim.2
  25.7 15.5 %all_to_all.15.feat = bf16[16,128,256]{2,1,0:T(8,128)(2,1)S(1)} all-to-all(bf16[16,128,256]{2,1,0:T(8,128)(2,1)S(1)} %bitcast.6), channel_id=1, replica_groups=mesh['x'=4,'zl'=4,'c'=2,'zh'=4,'y'=4] {'y'}, dimensions={0} | all-to-all | bytes 2097152 | tf_op jit(solution)/shard_map/all_to_all | solution.py:106
  41.2 0.0 copy-done.2
  41.2 0.0 copy-done.1
  41.2 5.3 %tile_products.1 = (f32[16,128,256]{2,1,0:T(8,128)S(1)}, bf16[16,128,256]{2,1,0:T(8,128)(2,1)S(1)}) custom-call(s32[128]{0:T(128)S(1)} %copy-done.1, s32[128]{0:T(128)S(1)} %copy-done.2, bf16[128,128,128]{2,1,0:T(8,128)(2,1)} %adj_hbm.1, bf16[16,128,256]{2,1,0:T(8,128)(2,1)S(1)} %all_to_all.15.feat), custom_call_target="tpu_custom_call" | custom-call | flops 1073741824 | bytes 4194304 | tf_op jit(solution)/shard_map/tile_products/pallas_call | solution.py:61
  46.4 6.5 %collective-permute-start = (bf16[16,128,256]{2,1,0:T(8,128)(2,1)S(1)}, bf16[16,128,256]{2,1,0:T(8,128)(2,1)S(1)}, u32[]{:S(2)}, u32[]{:S(2)}) collective-permute-start(bf16[16,128,256]{2,1,0:T(8,128)(2,1)S(1)} %get-tuple-element.8), channel_id=1, source_target_pairs={{0,16},{16,0},{1,17},{17,1},{2,18},{18,2},{3,19},{19,3},{4,20},{20... | collective-permute-start | bytes 3145736 | tf_op jit(solution)/shard_map/ppermute | solution.py:108
  52.9 2.3 %collective-permute-done = bf16[16,128,256]{2,1,0:T(8,128)(2,1)S(1)} collective-permute-done((bf16[16,128,256]{2,1,0:T(8,128)(2,1)S(1)}, bf16[16,128,256]{2,1,0:T(8,128)(2,1)S(1)}, u32[]{:S(2)}, u32[]{:S(2)}) %collective-permute-start) | collective-permute-done | bytes 1048608 | tf_op jit(solution)/shard_map/ppermute | solution.py:108
  55.2 0.3 add_convert_fusion
  55.5 17.5 %all_to_all.16 = bf16[16,128,256]{2,1,0:T(8,128)(2,1)S(1)} all-to-all(bf16[16,128,256]{2,1,0:T(8,128)(2,1)S(1)} %add_convert_fusion), channel_id=1, replica_groups={{0,128,256,384},{32,160,288,416},{64,192,320,448},{96,224,352,480},{16,..., dimensions={0} | all-to-all | bytes 2097152 | tf_op jit(solution)/shard_map/all_to_all | solution.py:87
  73.0 0.2 convert_element_type.26
  73.2 0.0 copy-start.3
  73.3 0.1 fusion.2
  73.4 9.3 %all_to_all.17 = bf16[4,128,256]{2,1,0:T(8,128)(2,1)S(1)} all-to-all(bf16[4,128,256]{2,1,0:T(8,128)(2,1)S(1)} %fusion.2), channel_id=1, replica_groups={{16,144,272,400},{48,176,304,432},{80,208,336,464},{112,240,368,496},{0..., dimensions={0} | all-to-all | bytes 524288 | tf_op jit(solution)/shard_map/all_to_all | solution.py:87
  82.8 0.0 copy-done
  82.8 0.0 copy-done.3
  82.8 0.8 fusion.1
  (1 shorter events, 0.0 us)
Async XLA Ops:
  0.0 82.8 %copy-start = (bf16[256,256]{1,0:T(8,128)(2,1)S(1)}, bf16[256,256]{1,0:T(8,128)(2,1)}, u32[]{:S(2)}) copy-start(bf16[256,256]{1,0:T(8,128)(2,1)} %param.10) | copy-start | bytes 393220
  0.0 41.2 %copy-start.2 = (s32[128]{0:T(128)S(1)}, s32[128]{0:T(128)}, u32[]{:S(2)}) copy-start(s32[128]{0:T(128)} %cols_ref.1) | copy-start | bytes 1540
  0.0 41.2 %copy-start.1 = (s32[128]{0:T(128)S(1)}, s32[128]{0:T(128)}, u32[]{:S(2)}) copy-start(s32[128]{0:T(128)} %rows_ref.1) | copy-start | bytes 1540
  46.4 8.8 %collective-permute-start = (bf16[16,128,256]{2,1,0:T(8,128)(2,1)S(1)}, bf16[16,128,256]{2,1,0:T(8,128)(2,1)S(1)}, u32[]{:S(2)}, u32[]{:S(2)}) collective-permute-start(bf16[16,128,256]{2,1,0:T(8,128)(2,1)S(1)} %get-tuple-element.8), channel_id=1, source_target_pairs={{0,16},{16,0},{1,17},{17,1},{2,18},{18,2},{3,19},{19,3},{4,20},{20... | collective-permute-start | bytes 3145736 | tf_op jit(solution)/shard_map/ppermute | solution.py:108
  73.2 9.5 %copy-start.3 = (f32[256]{0:T(256)S(1)}, f32[256]{0:T(256)}, u32[]{:S(2)}) copy-start(f32[256]{0:T(256)} %param.11) | copy-start | bytes 3076

commit v5 on v4

--- a/solution.py
+++ b/solution.py
@@ -7,8 +7,7 @@
 
 F32 = jnp.float32
 BF16 = jnp.bfloat16
-GROUP = 32
-PIECE = 8
+PIECES = ((0, 32), (32, 96))
 VMEM_LIMIT = 48 << 20
 
 
@@ -16,22 +15,19 @@
     rows_ref, cols_ref, adj_hbm, feat, own_ref, other_ref, acc, adj, sems
 ):
     half = own_ref.shape[0]
-    count = adj.shape[0]
     core = lax.axis_index("c")
 
     def fetch(i):
-        part = pl.ds(i * PIECE, PIECE)
+        part = pl.ds(*PIECES[i])
         return pltpu.make_async_copy(adj_hbm.at[part], adj.at[part], sems.at[i])
 
-    for i in range(count // PIECE):
+    for i in range(len(PIECES)):
         fetch(i).start()
     acc[...] = jnp.zeros_like(acc)
 
-    def run(first, size):
-        for i in range(size // PIECE):
-            fetch(first // PIECE + i).wait()
-        for k in range(size):
-            t = first + k
+    for i, (start, size) in enumerate(PIECES):
+        fetch(i).wait()
+        for t in range(start, start + size):
             row = rows_ref[t]
             col = cols_ref[t]
             to_x = row >> 3
@@ -40,13 +36,6 @@
             slot = ((row & 1) ^ core) * half + chip
             block = (col & 3) * 4 + (col >> 2)
             acc[slot] += jnp.dot(adj[t], feat[block], preferred_element_type=F32)
-
-    run(0, GROUP // 2)
-    run(GROUP // 2, GROUP // 2)
-
-    @pl.loop(1, count // GROUP)
-    def _(g):
-        run(g * GROUP, GROUP)
 
     own_ref[...] = acc[:half]
     other_ref[...] = acc[half:].astype(BF16)
@@ -69,7 +58,7 @@
         scratch_shapes=[
             pltpu.VMEM((2 * half, side, width), F32),
             pltpu.VMEM((count, side, side), BF16),
-            pltpu.SemaphoreType.DMA((count // PIECE,)),
+            pltpu.SemaphoreType.DMA((len(PIECES),)),
         ],
         cost_estimate=pl.CostEstimate(
             flops=2 * count * side * side * width,
@@ -93,10 +82,9 @@
         tiled=True,
     )
     share = blocks.shape[0] // 4
-    parts = arrived.astype(F32)
-    total = parts[:share]
+    total = arrived[:share].astype(F32)
     for i in range(1, 4):
-        total = total + parts[i * share : (i + 1) * share]
+        total = total + arrived[i * share : (i + 1) * share].astype(F32)
     return total
 
 

time: 83.8 us -> 83.4 us (level)
  no operation moved by 1% of the time
where the time goes in v5:
time: 83.4 us; the launch traced here: 83.2 us
  blocking collectives  67.9 us (81%)
  starting transfers between devices  6.48 us (8%)
  Pallas kernels  5.08 us (6%)
  waiting for transfers between devices  2.26 us (3%)
    all_to_all x2, blocking collectives, exchange(): lax.all_to_all(blocks.astype(BF16), ('x', 'zl', 'c'), 0, 0, axis_index_gr...  26.8 us
    all_gather x1, blocking collectives, on_device(): column = lax.all_gather(features, 'zh', axis=0)  25.6 us
    all_to_all x1, blocking collectives, on_device(): section = lax.all_to_all(copies, 'y', 0, 0, tiled=True)  15.5 us
    ppermute x1, starting transfers between devices, on_device(): received = lax.ppermute(other, 'c', [(0, 1), (1, 0)])  6.48 us
    pallas_call x1, Pallas kernels, tile_products(): pl.pallas_call(tile_kernel, out_shape=(jax.ShapeDtypeStruct((half, side,...  5.08 us
    ppermute x1, waiting for transfers between devices, on_device(): received = lax.ppermute(other, 'c', [(0, 1), (1, 0)])  2.26 us
  transfers between devices with their start and end apart: 1, of which 1 were waited for; matrix products, arithmetic and copies ran while one was open for 0% of the time, Pallas kernels for 0%

profile of v5, /device:TPU:1, one launch (start us, length us, event | category | flops | bytes accessed | tf_op | source)
XLA Modules:
  0.0 83.2 jit_solution(12968828049225700830)
XLA Ops:
  0.0 0.0 copy-start
  0.0 0.0 copy-start.2
  0.0 0.0 copy-start.1
  0.0 25.6 %all-gather = bf16[512,256]{1,0:T(8,128)(2,1)S(1)} all-gather(bf16[128,256]{1,0:T(8,128)(2,1)} %param.9), channel_id=2, replica_groups=mesh['x'=4,'zl'=4,'c'=2,'zh'=4,'y'=4] {'zh'}, dimensions={0}, use_global_device_ids=true | all-gather | bytes 327680 | tf_op jit(solution)/shard_map/all_gather | solution.py:92
  25.6 0.1 broadcast_in_dim.2
  25.7 15.5 %all_to_all.15.feat = bf16[16,128,256]{2,1,0:T(8,128)(2,1)S(1)} all-to-all(bf16[16,128,256]{2,1,0:T(8,128)(2,1)S(1)} %bitcast.6), channel_id=1, replica_groups=mesh['x'=4,'zl'=4,'c'=2,'zh'=4,'y'=4] {'y'}, dimensions={0} | all-to-all | bytes 2097152 | tf_op jit(solution)/shard_map/all_to_all | solution.py:94
  41.2 0.0 copy-done.2
  41.2 0.0 copy-done.1
  41.2 5.1 %tile_products.1 = (f32[16,128,256]{2,1,0:T(8,128)S(1)}, bf16[16,128,256]{2,1,0:T(8,128)(2,1)S(1)}) custom-call(s32[128]{0:T(128)S(1)} %copy-done.1, s32[128]{0:T(128)S(1)} %copy-done.2, bf16[128,128,128]{2,1,0:T(8,128)(2,1)} %adj_hbm.1, bf16[16,128,256]{2,1,0:T(8,128)(2,1)S(1)} %all_to_all.15.feat), custom_call_target="tpu_custom_call" | custom-call | flops 1073741824 | bytes 4194304 | tf_op jit(solution)/shard_map/tile_products/pallas_call | solution.py:50
  46.3 6.5 %collective-permute-start = (bf16[16,128,256]{2,1,0:T(8,128)(2,1)S(1)}, bf16[16,128,256]{2,1,0:T(8,128)(2,1)S(1)}, u32[]{:S(2)}, u32[]{:S(2)}) collective-permute-start(bf16[16,128,256]{2,1,0:T(8,128)(2,1)S(1)} %get-tuple-element.8), channel_id=1, source_target_pairs={{0,16},{16,0},{1,17},{17,1},{2,18},{18,2},{3,19},{19,3},{4,20},{20... | collective-permute-start | bytes 3145736 | tf_op jit(solution)/shard_map/ppermute | solution.py:96
  52.8 2.3 %collective-permute-done = bf16[16,128,256]{2,1,0:T(8,128)(2,1)S(1)} collective-permute-done((bf16[16,128,256]{2,1,0:T(8,128)(2,1)S(1)}, bf16[16,128,256]{2,1,0:T(8,128)(2,1)S(1)}, u32[]{:S(2)}, u32[]{:S(2)}) %collective-permute-start) | collective-permute-done | bytes 1048608 | tf_op jit(solution)/shard_map/ppermute | solution.py:96
  55.0 0.3 add_convert_fusion
  55.3 0.0 copy-start.3
  55.4 17.5 %all_to_all.16 = bf16[16,128,256]{2,1,0:T(8,128)(2,1)S(1)} all-to-all(bf16[16,128,256]{2,1,0:T(8,128)(2,1)S(1)} %add_convert_fusion), channel_id=1, replica_groups={{0,128,256,384},{32,160,288,416},{64,192,320,448},{96,224,352,480},{16,..., dimensions={0} | all-to-all | bytes 2097152 | tf_op jit(solution)/shard_map/all_to_all | solution.py:76
  72.9 0.1 add_convert_fusion.1
  73.0 9.3 %all_to_all.17 = bf16[4,128,256]{2,1,0:T(8,128)(2,1)S(1)} all-to-all(bf16[4,128,256]{2,1,0:T(8,128)(2,1)S(1)} %add_convert_fusion.1), channel_id=1, replica_groups={{16,144,272,400},{48,176,304,432},{80,208,336,464},{112,240,368,496},{0..., dimensions={0} | all-to-all | bytes 524288 | tf_op jit(solution)/shard_map/all_to_all | solution.py:76
  82.3 0.0 copy-done
  82.3 0.0 copy-done.3
  82.3 0.8 fusion.1
Async XLA Ops:
  0.0 82.3 %copy-start = (bf16[256,256]{1,0:T(8,128)(2,1)S(1)}, bf16[256,256]{1,0:T(8,128)(2,1)}, u32[]{:S(2)}) copy-start(bf16[256,256]{1,0:T(8,128)(2,1)} %param.10) | copy-start | bytes 393220
  0.0 41.2 %copy-start.2 = (s32[128]{0:T(128)S(1)}, s32[128]{0:T(128)}, u32[]{:S(2)}) copy-start(s32[128]{0:T(128)} %cols_ref.1) | copy-start | bytes 1540
  0.0 41.2 %copy-start.1 = (s32[128]{0:T(128)S(1)}, s32[128]{0:T(128)}, u32[]{:S(2)}) copy-start(s32[128]{0:T(128)} %rows_ref.1) | copy-start | bytes 1540
  46.3 8.8 %collective-permute-start = (bf16[16,128,256]{2,1,0:T(8,128)(2,1)S(1)}, bf16[16,128,256]{2,1,0:T(8,128)(2,1)S(1)}, u32[]{:S(2)}, u32[]{:S(2)}) collective-permute-start(bf16[16,128,256]{2,1,0:T(8,128)(2,1)S(1)} %get-tuple-element.8), channel_id=1, source_target_pairs={{0,16},{16,0},{1,17},{17,1},{2,18},{18,2},{3,19},{19,3},{4,20},{20... | collective-permute-start | bytes 3145736 | tf_op jit(solution)/shard_map/ppermute | solution.py:96
  55.3 27.0 %copy-start.3 = (f32[256]{0:T(256)S(1)}, f32[256]{0:T(256)}, u32[]{:S(2)}) copy-start(f32[256]{0:T(256)} %param.11) | copy-start | bytes 3076
